TPU v7x, 32 devices: a whole 2x2x4 slice. The times are simulated.
32 devices in a mesh: dp: 8 (over z, x), tensor: 4 (over y, core).
Axes of the slice: x: 2, y: 2, z: 4, core: 2. Of those that a mesh axis runs over, the one named last changes fastest.
Arguments:
- tokens: bfloat16 [16384, 768], P(('dp', 'tensor')), may hold values from -6 to 6
- w_query: bfloat16 [768, 768], P(None, 'tensor'), may hold values from -0.3125 to 0.3125
- w_key: bfloat16 [768, 768], P(None, 'tensor'), may hold values from -0.3125 to 0.3125
- w_value: bfloat16 [768, 768], P(None, 'tensor'), may hold values from -0.21875 to 0.21875
- b_query: bfloat16 [768], P('tensor'), may hold values from -3 to 3
- b_value: bfloat16 [768], P('tensor'), may hold values from -3 to 3
- w_output: bfloat16 [768, 768], P('tensor'), may hold values from -0.375 to 0.375
- b_output: bfloat16 [768], replicated, may hold values from -3 to 3
- first_gain: bfloat16 [768], replicated, may hold values from 0.5 to 1.5
- first_shift: bfloat16 [768], replicated, may hold values from -3 to 3
- w_up: bfloat16 [768, 3072], P(None, 'tensor'), may hold values from -0.21875 to 0.21875
- b_up: bfloat16 [3072], P('tensor'), may hold values from -3 to 3
- w_down: bfloat16 [3072, 768], P('tensor'), may hold values from -0.15625 to 0.15625
- b_down: bfloat16 [768], replicated, may hold values from -3 to 3
- second_gain: bfloat16 [768], replicated, may hold values from 0.5 to 1.5
- second_shift: bfloat16 [768], replicated, may hold values from -3 to 3
- cotangent: bfloat16 [16384, 768], P(('dp', 'tensor')), may hold values from -24 to 24, as said below
Outputs:
- layer_out: bfloat16 [16384, 768], P(('dp', 'tensor'))
- grad_tokens: bfloat16 [16384, 768], P(('dp', 'tensor'))
- grad_w_query: float32 [768, 768], P(None, 'tensor')
- grad_w_key: float32 [768, 768], P(None, 'tensor')
- grad_w_value: float32 [768, 768], P(None, 'tensor')
- grad_b_query: float32 [768], P('tensor')
- grad_b_value: float32 [768], P('tensor')
- grad_w_output: float32 [768, 768], P('tensor')
- grad_b_output: float32 [768], replicated
- grad_first_gain: float32 [768], replicated
- grad_first_shift: float32 [768], replicated
- grad_w_up: float32 [768, 3072], P(None, 'tensor')
- grad_b_up: float32 [3072], P('tensor')
- grad_w_down: float32 [3072, 768], P('tensor')
- grad_b_down: float32 [768], replicated
- grad_second_gain: float32 [768], replicated
- grad_second_shift: float32 [768], replicated
Inputs may be any that keep to these rules, and one draw needn't show every extreme that they name: cotangent of the layer's output.
All inputs are finite; a program needn't handle non-finite values.
Results may differ from a plain program's by a relative error of at most 0.013.
The roundings to bfloat16 on the way count: a program that leaves them out, or rounds other values in their place, can miss the bound.
Values may be sent and summed in bfloat16 or wider, within the bound.
No kernel may reach another device: no remote copies, remote signals or barrier semaphores. Data moves between devices by JAX's collectives and lax.ppermute only.
A program may use at most 128 MiB of HBM per device.

v0:
```python
import jax
import jax.numpy as jnp
from jax import lax
from jax.sharding import PartitionSpec as P

HEAD = 64
SEQ_LEN = 512


def layer_norm(values, gain_row, shift_row):
    center = values - jnp.mean(values, axis=-1, keepdims=True)
    spread = jnp.mean(center * center, axis=-1, keepdims=True)
    return center * lax.rsqrt(spread + 1e-12) * gain_row + shift_row


def gelu_exact(values):
    return jax.nn.gelu(values, approximate=False)


def contract_rows(left, right):
    return lax.dot_general(
        left, right, (((0,), (0,)), ((), ())), preferred_element_type=jnp.float32
    )


def contract_cols(left, right):
    return lax.dot_general(
        left, right, (((1,), (1,)), ((), ())), preferred_element_type=jnp.float32
    )


def attend_forward(packed):
    queries, key_rows, value_rows = packed
    scores = (
        jnp.einsum("qhd,khd->hqk", queries, key_rows, preferred_element_type=jnp.float32) * 0.125
    )
    highest = jnp.max(scores, axis=-1, keepdims=True)
    unnorm = jnp.exp(scores - highest)
    totals = jnp.sum(unnorm, axis=-1, keepdims=True)
    soft_probs = (unnorm / totals).astype(jnp.bfloat16)
    attended = jnp.einsum(
        "hqk,khd->qhd", soft_probs, value_rows, preferred_element_type=jnp.float32
    )
    return (attended.astype(jnp.bfloat16), highest + jnp.log(totals))


def attend_backward(packed):
    queries, key_rows, value_rows, grad_att, log_total = packed
    scores = (
        jnp.einsum("qhd,khd->hqk", queries, key_rows, preferred_element_type=jnp.float32) * 0.125
    )
    soft_probs = jnp.exp(scores - log_total)
    grad_prob = jnp.einsum("qhd,khd->hqk", grad_att, value_rows, preferred_element_type=jnp.float32)
    inner_sum = jnp.sum(soft_probs * grad_prob, axis=-1, keepdims=True)
    grad_score = (soft_probs * (grad_prob - inner_sum)).astype(jnp.bfloat16)
    grad_query = (
        jnp.einsum("hqk,khd->qhd", grad_score, key_rows, preferred_element_type=jnp.float32) * 0.125
    ).astype(jnp.bfloat16)
    grad_key = (
        jnp.einsum("hqk,qhd->khd", grad_score, queries, preferred_element_type=jnp.float32) * 0.125
    ).astype(jnp.bfloat16)
    grad_value = jnp.einsum(
        "hqk,qhd->khd",
        soft_probs.astype(jnp.bfloat16),
        grad_att,
        preferred_element_type=jnp.float32,
    ).astype(jnp.bfloat16)
    return (grad_query, grad_key, grad_value)


def on_device(
    tokens,
    w_query,
    w_key,
    w_value,
    b_query,
    b_value,
    w_output,
    b_output,
    first_gain,
    first_shift,
    w_up,
    b_up,
    w_down,
    b_down,
    second_gain,
    second_shift,
    cotangent,
):
    share_rows = tokens.shape[0]
    group_rows = share_rows * lax.axis_size("tensor")
    local_width = w_query.shape[1]
    local_heads = local_width // HEAD
    seq_count = group_rows // SEQ_LEN
    w_joined = jnp.concatenate([w_query, w_key, w_value], axis=1)
    b_joined = jnp.concatenate(
        [
            b_query.astype(jnp.float32),
            jnp.zeros((local_width,), jnp.float32),
            b_value.astype(jnp.float32),
        ]
    )

    def split_heads(block):
        return block.reshape(seq_count, SEQ_LEN, local_heads, HEAD)

    inputs_full = lax.all_gather(tokens, "tensor", axis=0, tiled=True)
    projected = (
        jnp.dot(inputs_full, w_joined, preferred_element_type=jnp.float32) + b_joined
    ).astype(jnp.bfloat16)
    queries = split_heads(projected[:, :local_width])
    key_rows = split_heads(projected[:, local_width : 2 * local_width])
    value_rows = split_heads(projected[:, 2 * local_width :])
    attended, log_total = lax.map(attend_forward, (queries, key_rows, value_rows))
    attended = attended.reshape(group_rows, local_width)
    picked = attended
    attention_part = lax.psum_scatter(
        jnp.dot(picked, w_output, preferred_element_type=jnp.float32),
        "tensor",
        scatter_dimension=0,
        tiled=True,
    )
    first_sum = attention_part + b_output.astype(jnp.float32) + tokens.astype(jnp.float32)
    normed, first_pull = jax.vjp(
        layer_norm, first_sum, first_gain.astype(jnp.float32), first_shift.astype(jnp.float32)
    )
    normed_low = normed.astype(jnp.bfloat16)
    normed_full = lax.all_gather(normed_low, "tensor", axis=0, tiled=True)
    up_rows = jnp.dot(normed_full, w_up, preferred_element_type=jnp.float32) + b_up.astype(
        jnp.float32
    )
    active, gelu_pull = jax.vjp(gelu_exact, up_rows)
    active = active.astype(jnp.bfloat16)
    picked = active
    feed_part = lax.psum_scatter(
        jnp.dot(picked, w_down, preferred_element_type=jnp.float32),
        "tensor",
        scatter_dimension=0,
        tiled=True,
    )
    second_sum = feed_part + b_down.astype(jnp.float32) + normed
    layer_out, second_pull = jax.vjp(
        layer_norm, second_sum, second_gain.astype(jnp.float32), second_shift.astype(jnp.float32)
    )
    grad_second, grad_second_gain, grad_second_shift = second_pull(cotangent.astype(jnp.float32))
    grad_b_down = jnp.sum(grad_second, axis=0)
    down_low = grad_second.astype(jnp.bfloat16)
    down_full = lax.all_gather(down_low, "tensor", axis=0, tiled=True)
    grad_w_down = contract_rows(active, down_full)
    grad_active = contract_cols(down_full, w_down)
    grad_up = gelu_pull(grad_active)[0].astype(jnp.bfloat16)
    grad_b_up = jnp.sum(grad_up, axis=0, dtype=jnp.float32)
    grad_w_up = contract_rows(normed_full, grad_up)
    picked = grad_up
    hidden_part = lax.psum_scatter(
        contract_cols(picked, w_up), "tensor", scatter_dimension=0, tiled=True
    )
    grad_normed = hidden_part + grad_second
    grad_first, grad_first_gain, grad_first_shift = first_pull(grad_normed)
    grad_b_output = jnp.sum(grad_first, axis=0)
    first_low = grad_first.astype(jnp.bfloat16)
    first_full = lax.all_gather(first_low, "tensor", axis=0, tiled=True)
    grad_w_output = contract_rows(attended, first_full)
    grad_att = contract_cols(first_full, w_output).astype(jnp.bfloat16)
    grad_query, grad_key, grad_value = lax.map(
        attend_backward, (queries, key_rows, value_rows, split_heads(grad_att), log_total)
    )
    grad_joined = jnp.concatenate(
        [
            grad_query.reshape(group_rows, local_width),
            grad_key.reshape(group_rows, local_width),
            grad_value.reshape(group_rows, local_width),
        ],
        axis=1,
    )
    grad_b_query = jnp.sum(grad_joined[:, :local_width], axis=0, dtype=jnp.float32)
    grad_b_value = jnp.sum(grad_joined[:, 2 * local_width :], axis=0, dtype=jnp.float32)
    grad_w_joined = contract_rows(inputs_full, grad_joined)
    picked = grad_joined
    input_part = lax.psum_scatter(
        contract_cols(picked, w_joined), "tensor", scatter_dimension=0, tiled=True
    )
    grad_tokens = (input_part + grad_first).astype(jnp.bfloat16)
    grad_w_query = grad_w_joined[:, :local_width]
    grad_w_key = grad_w_joined[:, local_width : 2 * local_width]
    grad_w_value = grad_w_joined[:, 2 * local_width :]
    (
        grad_w_query,
        grad_w_key,
        grad_w_value,
        grad_b_query,
        grad_b_value,
        grad_w_output,
        grad_w_up,
        grad_b_up,
        grad_w_down,
    ) = lax.psum(
        (
            grad_w_query,
            grad_w_key,
            grad_w_value,
            grad_b_query,
            grad_b_value,
            grad_w_output,
            grad_w_up,
            grad_b_up,
            grad_w_down,
        ),
        "dp",
    )
    (
        grad_b_output,
        grad_first_gain,
        grad_first_shift,
        grad_b_down,
        grad_second_gain,
        grad_second_shift,
    ) = lax.psum(
        (
            grad_b_output,
            grad_first_gain,
            grad_first_shift,
            grad_b_down,
            grad_second_gain,
            grad_second_shift,
        ),
        ("dp", "tensor"),
    )
    return (
        layer_out.astype(jnp.bfloat16),
        grad_tokens,
        grad_w_query,
        grad_w_key,
        grad_w_value,
        grad_b_query,
        grad_b_value,
        grad_w_output,
        grad_b_output,
        grad_first_gain,
        grad_first_shift,
        grad_w_up,
        grad_b_up,
        grad_w_down,
        grad_b_down,
        grad_second_gain,
        grad_second_shift,
    )


def solution(mesh):
    return jax.shard_map(
        on_device,
        mesh=mesh,
        in_specs=(
            P(("dp", "tensor"), None),
            P(None, "tensor"),
            P(None, "tensor"),
            P(None, "tensor"),
            P("tensor"),
            P("tensor"),
            P("tensor", None),
            P(),
            P(),
            P(),
            P(None, "tensor"),
            P("tensor"),
            P("tensor", None),
            P(),
            P(),
            P(),
            P(("dp", "tensor"), None),
        ),
        out_specs=(
            P(("dp", "tensor"), None),
            P(("dp", "tensor"), None),
            P(None, "tensor"),
            P(None, "tensor"),
            P(None, "tensor"),
            P("tensor"),
            P("tensor"),
            P("tensor", None),
            P(),
            P(),
            P(),
            P(None, "tensor"),
            P("tensor"),
            P("tensor", None),
            P(),
            P(),
            P(),
        ),
        check_vma=False,
    )
```

profile of v0, /device:TPU:0, one launch (start us, length us, event | category | flops | bytes accessed | tf_op | source)
XLA Modules:
  0.0 759.8 jit_solution(11368604049422810197)
XLA Ops:
  12.4 28.5 %all-gather.5.cloned.1.call-done = bf16[2048,768]{1,0:T(8,128)(2,1)} async-done(((bf16[512,768]{1,0:T(8,128)(2,1)}), bf16[2048,768]{1,0:T(8,128)(2,1)}) %all-gather.5.cloned.1.call-update) | async-done | bytes 3145744 | tf_op jit(solution)/shard_map/all_gather | solution.py:107
  40.9 3.9 fusion.63
  54.2 12.9 %while.26 = (s32[]{:T(128)}, bf16[4,512,3,64]{1,3,2,0:T(8,128)(2,1)}, f32[4,3,512,1]{2,1,3,0:T(4,128)}, bf16[4,512,3,64]{1,3,2,0:T(8,128)(2,1)S(1)}, bf16[4,512,...) while((s32[]{:T(128)}, bf16[4,512,3,64]{1,3,2,0:T(8,128)(2,1)}, ...), condition=%wide.region_3.4_spmd, body=%wide.region_0.3_spmd.sunk | while | flops 208501248 | bytes 10281549 | solution.py:114
  67.1 2.3 copy.52
  70.5 3.7 fusion.78
  74.9 57.8 %reduce-scatter.5.cloned.1.call-done = f32[512,768]{1,0:T(8,128)} async-done(((f32[2048,768]{1,0:T(8,128)}), f32[512,768]{1,0:T(8,128)}) %reduce-scatter.5.cloned.1.call-update) | async-done | bytes 1572880 | tf_op jit(solution)/shard_map/reduce_scatter | solution.py:117
  132.8 1.9 fusion.75
  137.9 27.7 %all-gather.7.cloned.1.call-done = bf16[2048,768]{1,0:T(8,128)(2,1)} async-done(((bf16[512,768]{1,0:T(8,128)(2,1)}), bf16[2048,768]{1,0:T(8,128)(2,1)}) %all-gather.7.cloned.1.call-update) | async-done | bytes 3145744 | tf_op jit(solution)/shard_map/all_gather | solution.py:128
  165.5 18.4 %multiply_convert_fusion.1 = (bf16[2048,768]{1,0:T(8,128)(2,1)S(1)}, f32[2048,768]{1,0:T(8,128)}, f32[2048,768]{1,0:T(8,128)}) fusion(f32[768]{0:T(1024)S(1)} %convert_element_type.116, bf16[2048,768]{1,0:T(8,128)(2,1)} %all-gather.7.cloned.1.call-done, bf16[768,768]{1,0:T(8,128)(2,1)S(1)} %copy-done), kind=kOutput, calls=%fused_computation.64 | convolution fusion | flops 2519728128 | bytes 20057088 | tf_op jit(solution)/shard_map/dot_general | solution.py:129
  185.7 4.5 fusion.79
  193.4 55.3 %reduce-scatter.7.cloned.1.call-done = f32[512,768]{1,0:T(8,128)} async-done(((f32[2048,768]{1,0:T(8,128)}), f32[512,768]{1,0:T(8,128)}) %reduce-scatter.7.cloned.1.call-update) | async-done | bytes 1572880 | tf_op jit(solution)/shard_map/reduce_scatter | solution.py:135
  248.7 2.0 fusion.73
  257.3 28.1 %all-gather.9.cloned.1.call-done = bf16[2048,768]{1,0:T(8,128)(2,1)} async-done(((bf16[512,768]{1,0:T(8,128)(2,1)}), bf16[2048,768]{1,0:T(8,128)(2,1)}) %all-gather.9.cloned.1.call-update) | async-done | bytes 3145744 | tf_op jit(solution)/shard_map/all_gather | solution.py:148
  285.4 11.0 %convert_reduce_fusion = (f32[768]{0:T(1024)}, bf16[2048,768]{1,0:T(8,128)(2,1)S(1)}) fusion(f32[2048,768]{1,0:T(8,128)} %get-tuple-element.195, f32[2048,768]{1,0:T(8,128)} %get-tuple-element.213, f32[768]{0:T(1024)} %copy-done.32, bf16[2048,768]{1,0:T(8,128)(2,1)} %all-gather.9.cloned.1.call-done, bf16[768,768]{1,0:T(8,128)(2,1)} %param.33), kind=kOutput, calls=%fused_computation.62 | convolution fusion | flops 2442657024 | bytes 20060160 | tf_op jit(solution)/shard_map/dot_general | solution.py:27
  298.1 4.5 fusion.80
  302.7 58.5 %reduce-scatter.9.cloned.1.call-done = f32[512,768]{1,0:T(8,128)} async-done(((f32[2048,768]{1,0:T(8,128)}), f32[512,768]{1,0:T(8,128)}) %reduce-scatter.9.cloned.1.call-update) | async-done | bytes 1572880 | tf_op jit(solution)/shard_map/reduce_scatter | solution.py:155
  361.2 3.3 multiply_reduce_fusion.2
  367.7 28.5 %all-gather.11.cloned.1.call-done = bf16[2048,768]{1,0:T(8,128)(2,1)} async-done(((bf16[512,768]{1,0:T(8,128)(2,1)}), bf16[2048,768]{1,0:T(8,128)(2,1)}) %all-gather.11.cloned.1.call-update) | async-done | bytes 3145744 | tf_op jit(solution)/shard_map/all_gather | solution.py:162
  396.2 3.1 convolution_convert_fusion
  402.0 27.8 %while.27 = (s32[]{:T(128)}, bf16[4,512,3,64]{1,3,2,0:T(8,128)(2,1)S(1)}, bf16[4,512,3,64]{1,3,2,0:T(8,128)(2,1)}, bf16[4,512,3,64]{1,3,2,0:T(8,128)(2,1)}, bf16...) while((s32[]{:T(128)}, ...), condition=%wide.region_17.18_spmd, body=%wide.region_15.17_spmd.sunk | while | flops 513243648 | bytes 25611368 | solution.py:165
  431.7 1.8 copy.59
  435.3 4.6 fusion.81
  440.2 7.0 fusion.84
  447.2 4.2 fusion.83
  451.4 2.0 convolution_bitcast_fusion
  457.4 40.8 %all-reduce = (f32[768]{0:T(1024)}, f32[768]{0:T(1024)}, f32[768]{0:T(1024)}, f32[768]{0:T(1024)}, f32[768]{0:T(1024)}, /*index=5*/f32[768]{0:T(1024)}) all-reduce(f32[768]{0:T(1024)S(1)} %get-tuple-element.211, f32[768]{0:T(1024)S(1)} %copy-done.29, f32[768]{0:T(1024)S(1)} %copy-done.30, ...), channel_id=1, replica_groups=mesh['dp'=8,'tensor'=4] {'dp','tensor'}, use_global_device_ids=true, to_apply=%region_28.29 | all-reduce | flops 4608 | bytes 36864 | tf_op jit(solution)/shard_map/psum | solution.py:218
  499.9 22.2 %all-reduce.1 = (f32[192]{0:T(256)}, f32[192]{0:T(256)}, f32[768]{0:T(1024)}) all-reduce(f32[192]{0:T(256)S(1)} %reduce_sum.216, f32[192]{0:T(256)S(1)} %reduce_sum.218, f32[768]{0:T(1024)S(1)} %copy-done.31), channel_id=1, replica_groups=mesh['dp'=8,'tensor'=4] {'dp'}, use_global_device_ids=true, to_apply=%region_23.24 | all-reduce | flops 1152 | bytes 9216 | tf_op jit(solution)/shard_map/psum | solution.py:197
  522.1 2.5 add_convert_fusion.2
  524.6 218.8 %all-reduce.5.cloned.1.call-done = (f32[768,192]{0,1:T(8,128)}, f32[768,192]{0,1:T(8,128)}, f32[768,192]{0,1:T(8,128)}, f32[192,768]{1,0:T(8,128)}, f32[768,768]{1,0:T(8,128)}, /*index=5*/f32[768,768]{1,0:T(8,128)}) async-done(((f32[768,192]{0,1:T(8,128)}, f32[768,192]{0,1:T(8,128)}, f32[768,192]{0,1:T(8,128)}, f32[192,768]{1,0:T(8,128)}, f32[768,768]{1,0:T(8,128)}, /*index=5*/f32[768,768]{1,0:T(8,128)}), ...) | async-done | bytes 7077904 | tf_op jit(solution)/shard_map/psum | solution.py:197
  743.5 2.1 copy.106
  745.5 1.9 copy.107
  747.4 1.9 copy.108
  (210 shorter events, 92.2 us)
Async XLA Ops:
  7.2 158.3 %copy-start = (bf16[768,768]{1,0:T(8,128)(2,1)S(1)}, bf16[768,768]{1,0:T(8,128)(2,1)}, u32[]{:S(2)}) copy-start(bf16[768,768]{1,0:T(8,128)(2,1)} %param.31) | copy-start | bytes 3538948
  7.2 33.7 %all-gather.5.cloned.1.call-start = ((), (), s32[]{:S(2)}) async-start(), calls=%async_computation.4 | async-start | bytes 3932160 | tf_op jit(solution)/shard_map/all_gather | solution.py:107
  7.9 124.8 %reduce-scatter.5.cloned.1.call-start = ((), (), s32[]{:S(2)}) async-start(), calls=%async_computation.5 | async-start | bytes 7864320 | tf_op jit(solution)/shard_map/reduce_scatter | solution.py:117
  12.4 28.5 %copy-start.20 = (bf16[768,576]{0,1:T(8,128)(2,1)}, bf16[768,576]{0,1:T(8,128)(2,1)S(1)}, u32[]{:S(2)}) copy-start(bf16[768,576]{0,1:T(8,128)(2,1)S(1)} %constant_dynamic-update-slice_fusion) | copy-start | bytes 2654212
  67.1 7.1 copy-start.2
  67.1 7.1 copy-start.9
  67.1 3.4 copy-start.16
  74.3 91.3 %all-gather.7.cloned.1.call-start = ((), (), s32[]{:S(2)}) async-start(), calls=%async_computation.6 | async-start | bytes 3932160 | tf_op jit(solution)/shard_map/all_gather | solution.py:128
  74.9 61.9 %copy-start.22 = (f32[768]{0:T(1024)}, f32[768]{0:T(1024)S(1)}, u32[]{:S(2)}) copy-start(f32[768]{0:T(1024)S(1)} %convert_element_type.114) | copy-start | bytes 9220
  136.8 111.9 %reduce-scatter.7.cloned.1.call-start = ((), (), s32[]{:S(2)}) async-start(), calls=%async_computation.7 | async-start | bytes 7864320 | tf_op jit(solution)/shard_map/reduce_scatter | solution.py:135
  137.9 46.1 %copy-start.32 = (f32[768]{0:T(1024)}, f32[768]{0:T(1024)S(1)}, u32[]{:S(2)}) copy-start(f32[768]{0:T(1024)S(1)} %convert_element_type.116) | copy-start | bytes 9220
  165.5 20.2 %copy-start.39 = (bf16[768,768]{1,0:T(8,128)(2,1)S(1)}, bf16[768,768]{1,0:T(8,128)(2,1)}, u32[]{:S(2)}) copy-start(bf16[768,768]{1,0:T(8,128)(2,1)} %param.33) | copy-start | bytes 3538948
  190.2 95.3 %all-gather.9.cloned.1.call-start = ((), (), s32[]{:S(2)}) async-start(), calls=%async_computation.8 | async-start | bytes 3932160 | tf_op jit(solution)/shard_map/all_gather | solution.py:148
  248.7 2.4 copy-start.11
  256.7 104.5 %reduce-scatter.9.cloned.1.call-start = ((), (), s32[]{:S(2)}) async-start(), calls=%async_computation.9 | async-start | bytes 7864320 | tf_op jit(solution)/shard_map/reduce_scatter | solution.py:155
  302.7 61.8 %copy-start.24 = (f32[512]{0:T(512)S(1)}, f32[512]{0:T(512)}, u32[]{:S(2)}) copy-start(f32[512]{0:T(512)} %copy-done.23) | copy-start | bytes 6148
  302.7 93.5 %all-gather.11.cloned.1.call-start = ((), (), s32[]{:S(2)}) async-start(), calls=%async_computation.10 | async-start | bytes 3932160 | tf_op jit(solution)/shard_map/all_gather | solution.py:162
  364.5 31.7 %copy-start.17 = (bf16[192,768]{1,0:T(8,128)(2,1)S(1)}, bf16[192,768]{1,0:T(8,128)(2,1)}, u32[]{:S(2)}) copy-start(bf16[192,768]{1,0:T(8,128)(2,1)} %param.27) | copy-start | bytes 884740
  367.5 154.6 %reduce-scatter.11.cloned.1.call-start = ((), (), s32[]{:S(2)}) async-start(), calls=%async_computation.11 | async-start | bytes 7864320 | tf_op jit(solution)/shard_map/reduce_scatter | solution.py:180
  399.2 2.7 copy-start.3
  431.7 3.6 copy-start.21
  439.9 303.6 %all-reduce.5.cloned.1.call-start = ((), (), s32[]{:S(2)}) async-start(), calls=%async_computation.12 | async-start | bytes 14155776 | tf_op jit(solution)/shard_map/psum | solution.py:197
  440.1 7.1 copy-start.38
  440.2 7.1 copy-start.42
  447.2 4.2 copy-start.19
  447.2 4.2 copy-start.37
  451.4 3.3 copy-start.10
  456.7 43.1 %copy-start.31 = (f32[768]{0:T(1024)S(1)}, f32[768]{0:T(1024)}, u32[]{:S(2)}) copy-start(f32[768]{0:T(1024)} %get-tuple-element.185) | copy-start | bytes 9220
  456.7 65.4 %copy-start.5 = (f32[512,768]{1,0:T(8,128)S(1)}, f32[512,768]{1,0:T(8,128)}, u32[]{:S(2)}) copy-start(f32[512,768]{1,0:T(8,128)} %copy-done.4) | copy-start | bytes 4718596
  743.5 5.9 copy-start.15
  743.5 6.7 copy-start.14
  750.2 2.8 copy-start.1
  (20 other events, 21.5 us)
Sparse Core Ops, SparseCore 0:
  9.6 31.2 all-gather.4
  74.4 58.3 reduce-scatter.4
  137.0 28.5 all-gather.6
  190.3 58.3 reduce-scatter.6
  256.9 28.5 all-gather.8
  302.8 58.3 reduce-scatter.8
  367.6 28.5 all-gather.10
  440.0 59.7 reduce-scatter.10
  506.0 237.3 all-reduce.4
where the time goes:
time: 768 us; the launch traced here: 760 us
  waiting for transfers between devices  504 us (66%)
  matrix products  98.3 us (13%)
  blocking collectives  63.1 us (8%)
  local copies, waits for them, and re-layouts  46.3 us (6%)
  other arithmetic  31.9 us (4%)
  between operations  14.5 us (2%)
    psum x1, waiting for transfers between devices, on_device(): lax.psum((grad_w_query, grad_w_key, grad_w_value, grad_b_query, grad_b_va...  219 us
    reduce_scatter x1, waiting for transfers between devices, on_device(): lax.psum_scatter(contract_cols(picked, w_up), 'tensor', scatter_dimension...  58.5 us
    reduce_scatter x1, waiting for transfers between devices, on_device(): lax.psum_scatter(jnp.dot(picked, w_output, preferred_element_type=jnp.flo...  57.8 us
    reduce_scatter x1, waiting for transfers between devices, on_device(): lax.psum_scatter(jnp.dot(picked, w_down, preferred_element_type=jnp.float...  55.3 us
    psum x1, blocking collectives, on_device(): lax.psum((grad_b_output, grad_first_gain, grad_first_shift, grad_b_down,...  40.8 us
    all_gather x1, waiting for transfers between devices, on_device(): inputs_full = lax.all_gather(tokens, 'tensor', axis=0, tiled=True)  28.5 us
    all_gather x1, waiting for transfers between devices, on_device(): first_full = lax.all_gather(first_low, 'tensor', axis=0, tiled=True)  28.5 us
    all_gather x1, waiting for transfers between devices, on_device(): down_full = lax.all_gather(down_low, 'tensor', axis=0, tiled=True)  28.1 us
  transfers between devices with their start and end apart: 9, of which 8 were waited for; matrix products, arithmetic and copies ran while one was open for 4% of the time, Pallas kernels for 0%

commit v1 on v0

--- a/solution.py
+++ b/solution.py
@@ -159,7 +159,15 @@
     grad_first, grad_first_gain, grad_first_shift = first_pull(grad_normed)
     grad_b_output = jnp.sum(grad_first, axis=0)
     first_low = grad_first.astype(jnp.bfloat16)
-    first_full = lax.all_gather(first_low, "tensor", axis=0, tiled=True)
+    ways, here, step = (lax.axis_size("tensor"), lax.axis_index("tensor"), first_low.shape[0])
+    line, have = (first_low, 1)
+    while have < ways:
+        line = jnp.concatenate(
+            [line, lax.ppermute(line, "tensor", [(d, (d - have) % ways) for d in range(ways)])],
+            axis=0,
+        )
+        have = 2 * have
+    first_full = jnp.roll(line, here * step, axis=0)
     grad_w_output = contract_rows(attended, first_full)
     grad_att = contract_cols(first_full, w_output).astype(jnp.bfloat16)
     grad_query, grad_key, grad_value = lax.map(

time: 768 us -> 793 us (1.033)
  waiting for transfers between devices: 504 us -> 518 us
    ppermute x0 -> x2, waiting for transfers between devices: none -> 43.9 us  [on_device(): lax.ppermute(line, 'tensor', [(d, (d - have) % ways) for d in range(ways)])]
    all_gather x1 -> x0, waiting for transfers between devices: 28.5 us -> none  [on_device(): first_full = lax.all_gather(first_low, 'tensor', axis=0, tiled=True)]
    psum x1, waiting for transfers between devices: 219 us -> 198 us  [on_device(): lax.psum((grad_w_query, grad_w_key, grad_w_value, grad_b_query, grad_b_va...]
    reduce_scatter x1, waiting for transfers between devices: 0.01 us -> 19.8 us  [on_device(): lax.psum_scatter(contract_cols(picked, w_joined), 'tensor', scatter_dimen...]
  transfers between devices with their start and end apart: 9 -> 10, of which waited for: 8 -> 10; matrix products, arithmetic and copies ran while one was open for 4% -> 4% of each run, Pallas kernels for 0% -> 0%
where the time goes in v1:
time: 793 us; the launch traced here: 786 us
  waiting for transfers between devices  518 us (65%)
  matrix products  98.5 us (12%)
  blocking collectives  66.7 us (8%)
  local copies, waits for them, and re-layouts  52.1 us (7%)
  other arithmetic  32.3 us (4%)
  between operations  14.8 us (2%)
    psum x1, waiting for transfers between devices, on_device(): lax.psum((grad_w_query, grad_w_key, grad_w_value, grad_b_query, grad_b_va...  198 us
    reduce_scatter x1, waiting for transfers between devices, on_device(): lax.psum_scatter(contract_cols(picked, w_up), 'tensor', scatter_dimension...  58.5 us
    reduce_scatter x1, waiting for transfers between devices, on_device(): lax.psum_scatter(jnp.dot(picked, w_output, preferred_element_type=jnp.flo...  57.8 us
    reduce_scatter x1, waiting for transfers between devices, on_device(): lax.psum_scatter(jnp.dot(picked, w_down, preferred_element_type=jnp.float...  55.2 us
    psum x1, blocking collectives, on_device(): lax.psum((grad_b_output, grad_first_gain, grad_first_shift, grad_b_down,...  44.3 us
    ppermute x2, waiting for transfers between devices, on_device(): lax.ppermute(line, 'tensor', [(d, (d - have) % ways) for d in range(ways)])  43.9 us
    all_gather x1, waiting for transfers between devices, on_device(): inputs_full = lax.all_gather(tokens, 'tensor', axis=0, tiled=True)  28.5 us
    all_gather x1, waiting for transfers between devices, on_device(): down_full = lax.all_gather(down_low, 'tensor', axis=0, tiled=True)  28.1 us
  transfers between devices with their start and end apart: 10, of which 10 were waited for; matrix products, arithmetic and copies ran while one was open for 4% of the time, Pallas kernels for 0%

profile of v1, /device:TPU:0, one launch (start us, length us, event | category | flops | bytes accessed | tf_op | source)
XLA Modules:
  0.0 785.5 jit_solution(2233453194579506255)
XLA Ops:
  12.4 28.5 %all-gather.4.cloned.1.call-done = bf16[2048,768]{1,0:T(8,128)(2,1)} async-done(((bf16[512,768]{1,0:T(8,128)(2,1)}), bf16[2048,768]{1,0:T(8,128)(2,1)}) %all-gather.4.cloned.1.call-update) | async-done | bytes 3145744 | tf_op jit(solution)/shard_map/all_gather | solution.py:107
  40.9 3.9 fusion.63
  54.1 12.9 %while.26 = (s32[]{:T(128)}, bf16[4,512,3,64]{1,3,2,0:T(8,128)(2,1)}, f32[4,3,512,1]{2,1,3,0:T(4,128)}, bf16[4,512,3,64]{1,3,2,0:T(8,128)(2,1)S(1)}, bf16[4,512,...) while((s32[]{:T(128)}, bf16[4,512,3,64]{1,3,2,0:T(8,128)(2,1)}, ...), condition=%wide.region_3.4_spmd, body=%wide.region_0.3_spmd.sunk | while | flops 208501248 | bytes 10281049 | solution.py:114
  67.1 2.3 copy.52
  70.5 3.7 fusion.87
  74.9 57.8 %reduce-scatter.5.cloned.1.call-done = f32[512,768]{1,0:T(8,128)} async-done(((f32[2048,768]{1,0:T(8,128)}), f32[512,768]{1,0:T(8,128)}) %reduce-scatter.5.cloned.1.call-update) | async-done | bytes 1572880 | tf_op jit(solution)/shard_map/reduce_scatter | solution.py:117
  137.9 27.7 %all-gather.6.cloned.1.call-done = bf16[2048,768]{1,0:T(8,128)(2,1)} async-done(((bf16[512,768]{1,0:T(8,128)(2,1)}), bf16[2048,768]{1,0:T(8,128)(2,1)}) %all-gather.6.cloned.1.call-update) | async-done | bytes 3145744 | tf_op jit(solution)/shard_map/all_gather | solution.py:128
  165.5 18.4 %multiply_convert_fusion.1 = (bf16[2048,768]{1,0:T(8,128)(2,1)S(1)}, f32[2048,768]{1,0:T(8,128)}, f32[2048,768]{1,0:T(8,128)}) fusion(f32[768]{0:T(1024)S(1)} %convert_element_type.116, bf16[2048,768]{1,0:T(8,128)(2,1)} %all-gather.6.cloned.1.call-done, bf16[768,768]{1,0:T(8,128)(2,1)S(1)} %copy-done), kind=kOutput, calls=%fused_computation.64 | convolution fusion | flops 2519728128 | bytes 20057088 | tf_op jit(solution)/shard_map/dot_general | solution.py:129
  185.7 4.5 fusion.88
  193.5 55.2 %reduce-scatter.7.cloned.1.call-done = f32[512,768]{1,0:T(8,128)} async-done(((f32[2048,768]{1,0:T(8,128)}), f32[512,768]{1,0:T(8,128)}) %reduce-scatter.7.cloned.1.call-update) | async-done | bytes 1572880 | tf_op jit(solution)/shard_map/reduce_scatter | solution.py:135
  248.7 2.0 fusion.82
  257.3 28.1 %all-gather.8.cloned.1.call-done = bf16[2048,768]{1,0:T(8,128)(2,1)} async-done(((bf16[512,768]{1,0:T(8,128)(2,1)}), bf16[2048,768]{1,0:T(8,128)(2,1)}) %all-gather.8.cloned.1.call-update) | async-done | bytes 3145744 | tf_op jit(solution)/shard_map/all_gather | solution.py:148
  285.4 11.0 %convert_reduce_fusion = (f32[768]{0:T(1024)}, bf16[2048,768]{1,0:T(8,128)(2,1)S(1)}) fusion(f32[2048,768]{1,0:T(8,128)} %get-tuple-element.197, f32[2048,768]{1,0:T(8,128)} %get-tuple-element.215, f32[768]{0:T(1024)} %copy-done.29, bf16[2048,768]{1,0:T(8,128)(2,1)} %all-gather.8.cloned.1.call-done, bf16[768,768]{1,0:T(8,128)(2,1)} %param.33), kind=kOutput, calls=%fused_computation.62 | convolution fusion | flops 2442657024 | bytes 20060160 | tf_op jit(solution)/shard_map/dot_general | solution.py:27
  298.1 4.5 fusion.89
  302.7 58.5 %reduce-scatter.9.cloned.1.call-done = f32[512,768]{1,0:T(8,128)} async-done(((f32[2048,768]{1,0:T(8,128)}), f32[512,768]{1,0:T(8,128)}) %reduce-scatter.9.cloned.1.call-update) | async-done | bytes 1572880 | tf_op jit(solution)/shard_map/reduce_scatter | solution.py:155
  361.2 2.7 multiply_reduce_fusion.2
  366.0 9.5 %collective-permute-done = bf16[512,768]{1,0:T(8,128)(2,1)S(1)} collective-permute-done((bf16[512,768]{1,0:T(8,128)(2,1)S(1)}, bf16[512,768]{1,0:T(8,128)(2,1)S(1)}, u32[]{:S(2)}, u32[]{:S(2)}) %collective-permute-start) | collective-permute-done | bytes 786464 | tf_op jit(solution)/shard_map/ppermute | solution.py:166
  379.1 34.4 %collective-permute-done.1 = bf16[1024,768]{1,0:T(8,128)(2,1)} collective-permute-done((bf16[1024,768]{1,0:T(8,128)(2,1)}, bf16[1024,768]{1,0:T(8,128)(2,1)}, u32[]{:S(2)}, u32[]{:S(2)}) %collective-permute-start.1) | collective-permute-done | bytes 1572896 | tf_op jit(solution)/shard_map/ppermute | solution.py:166
  413.5 2.8 constant_dynamic-update-slice_fusion.6
  418.2 2.7 constant_dynamic-update-slice_fusion.3
  420.9 3.0 fusion.68
  426.7 27.8 %while.27 = (s32[]{:T(128)}, bf16[4,512,3,64]{1,3,2,0:T(8,128)(2,1)}, bf16[4,512,3,64]{1,3,2,0:T(8,128)(2,1)}, bf16[4,512,3,64]{1,3,2,0:T(8,128)(2,1)S(1)}, bf16...) while((s32[]{:T(128)}, ...), condition=%wide.region_17.18_spmd, body=%wide.region_15.17_spmd.sunk | while | flops 513243648 | bytes 25611376 | solution.py:173
  459.6 4.6 fusion.90
  464.5 7.2 fusion.92
  471.8 4.2 fusion.91
  478.2 2.0 convolution_bitcast_fusion
  482.1 22.4 %all-reduce.1 = (f32[192]{0:T(256)}, f32[192]{0:T(256)}, f32[768]{0:T(1024)}) all-reduce(f32[192]{0:T(256)S(1)} %reduce_sum.216, f32[192]{0:T(256)S(1)} %reduce_sum.218, f32[768]{0:T(1024)S(1)} %copy-done.28), channel_id=1, replica_groups=mesh['dp'=8,'tensor'=4] {'dp'}, use_global_device_ids=true, to_apply=%region_23.24 | all-reduce | flops 1152 | bytes 9216 | tf_op jit(solution)/shard_map/psum | solution.py:205
  504.5 19.8 %reduce-scatter.11.cloned.1.call-done = f32[512,768]{1,0:T(8,128)} async-done(((f32[2048,768]{1,0:T(8,128)}), f32[512,768]{1,0:T(8,128)}) %reduce-scatter.11.cloned.1.call-update) | async-done | bytes 1572880 | tf_op jit(solution)/shard_map/reduce_scatter | solution.py:188
  524.3 2.5 add_reduce_fusion
  526.8 44.3 %all-reduce = (f32[768]{0:T(1024)}, f32[768]{0:T(1024)}, f32[768]{0:T(1024)}, f32[768]{0:T(1024)}, f32[768]{0:T(1024)}, /*index=5*/f32[768]{0:T(1024)}) all-reduce(f32[768]{0:T(1024)S(1)} %get-tuple-element.213, f32[768]{0:T(1024)S(1)} %get-tuple-element.134, ...), channel_id=1, replica_groups=mesh['dp'=8,'tensor'=4] {'dp','tensor'}, use_global_device_ids=true, to_apply=%region_28.29 | all-reduce | flops 4608 | bytes 36864 | tf_op jit(solution)/shard_map/psum | solution.py:226
  571.1 197.8 %all-reduce.5.cloned.1.call-done = (f32[768,192]{0,1:T(8,128)}, f32[768,192]{0,1:T(8,128)}, f32[768,192]{0,1:T(8,128)}, f32[192,768]{1,0:T(8,128)}, f32[768,768]{1,0:T(8,128)}, /*index=5*/f32[768,768]{1,0:T(8,128)}) async-done(((f32[768,192]{0,1:T(8,128)}, f32[768,192]{0,1:T(8,128)}, f32[768,192]{0,1:T(8,128)}, f32[192,768]{1,0:T(8,128)}, f32[768,768]{1,0:T(8,128)}, /*index=5*/f32[768,768]{1,0:T(8,128)}), ...) | async-done | bytes 7077904 | tf_op jit(solution)/shard_map/psum | solution.py:205
  768.9 2.1 copy.111
  (214 shorter events, 102.5 us)
Async XLA Ops:
  7.2 158.3 %copy-start = (bf16[768,768]{1,0:T(8,128)(2,1)S(1)}, bf16[768,768]{1,0:T(8,128)(2,1)}, u32[]{:S(2)}) copy-start(bf16[768,768]{1,0:T(8,128)(2,1)} %param.31) | copy-start | bytes 3538948
  7.2 33.7 %all-gather.4.cloned.1.call-start = ((), (), s32[]{:S(2)}) async-start(), calls=%async_computation.4 | async-start | bytes 3932160 | tf_op jit(solution)/shard_map/all_gather | solution.py:107
  7.9 124.8 %reduce-scatter.5.cloned.1.call-start = ((), (), s32[]{:S(2)}) async-start(), calls=%async_computation.5 | async-start | bytes 7864320 | tf_op jit(solution)/shard_map/reduce_scatter | solution.py:117
  12.4 28.5 %copy-start.19 = (bf16[768,576]{0,1:T(8,128)(2,1)}, bf16[768,576]{0,1:T(8,128)(2,1)S(1)}, u32[]{:S(2)}) copy-start(bf16[768,576]{0,1:T(8,128)(2,1)S(1)} %constant_dynamic-update-slice_fusion) | copy-start | bytes 2654212
  67.1 7.2 copy-start.2
  67.1 7.2 copy-start.10
  74.3 91.3 %all-gather.6.cloned.1.call-start = ((), (), s32[]{:S(2)}) async-start(), calls=%async_computation.6 | async-start | bytes 3932160 | tf_op jit(solution)/shard_map/all_gather | solution.py:128
  74.9 61.9 %copy-start.21 = (f32[768]{0:T(1024)}, f32[768]{0:T(1024)S(1)}, u32[]{:S(2)}) copy-start(f32[768]{0:T(1024)S(1)} %convert_element_type.114) | copy-start | bytes 9220
  136.8 111.9 %reduce-scatter.7.cloned.1.call-start = ((), (), s32[]{:S(2)}) async-start(), calls=%async_computation.7 | async-start | bytes 7864320 | tf_op jit(solution)/shard_map/reduce_scatter | solution.py:135
  137.9 46.1 %copy-start.29 = (f32[768]{0:T(1024)}, f32[768]{0:T(1024)S(1)}, u32[]{:S(2)}) copy-start(f32[768]{0:T(1024)S(1)} %convert_element_type.116) | copy-start | bytes 9220
  165.5 20.2 %copy-start.35 = (bf16[768,768]{1,0:T(8,128)(2,1)S(1)}, bf16[768,768]{1,0:T(8,128)(2,1)}, u32[]{:S(2)}) copy-start(bf16[768,768]{1,0:T(8,128)(2,1)} %param.33) | copy-start | bytes 3538948
  190.2 95.3 %all-gather.8.cloned.1.call-start = ((), (), s32[]{:S(2)}) async-start(), calls=%async_computation.8 | async-start | bytes 3932160 | tf_op jit(solution)/shard_map/all_gather | solution.py:148
  256.7 104.4 %reduce-scatter.9.cloned.1.call-start = ((), (), s32[]{:S(2)}) async-start(), calls=%async_computation.9 | async-start | bytes 7864320 | tf_op jit(solution)/shard_map/reduce_scatter | solution.py:155
  302.7 61.2 %copy-start.23 = (f32[512]{0:T(512)S(1)}, f32[512]{0:T(512)}, u32[]{:S(2)}) copy-start(f32[512]{0:T(512)} %copy-done.22) | copy-start | bytes 6148
  302.7 221.6 %reduce-scatter.11.cloned.1.call-start = ((), (), s32[]{:S(2)}) async-start(), calls=%async_computation.10 | async-start | bytes 7864320 | tf_op jit(solution)/shard_map/reduce_scatter | solution.py:188
  364.5 12.2 %copy-start.4 = (f32[512,768]{1,0:T(8,128)}, f32[512,768]{1,0:T(8,128)S(1)}, u32[]{:S(2)}) copy-start(f32[512,768]{1,0:T(8,128)S(1)} %get-tuple-element.190) | copy-start | bytes 4718596
  365.8 9.7 %collective-permute-start = (bf16[512,768]{1,0:T(8,128)(2,1)S(1)}, bf16[512,768]{1,0:T(8,128)(2,1)S(1)}, u32[]{:S(2)}, u32[]{:S(2)}) collective-permute-start(bf16[512,768]{1,0:T(8,128)(2,1)S(1)} %get-tuple-element.188), channel_id=1, source_target_pairs={{0,3},{1,0},{2,1},{3,2},{4,7},{5,4},{6,5},{7,6},{8,11},{9,8},{10,9... | collective-permute-start | bytes 2359304 | tf_op jit(solution)/shard_map/ppermute | solution.py:166
  376.7 36.8 %collective-permute-start.1 = (bf16[1024,768]{1,0:T(8,128)(2,1)}, bf16[1024,768]{1,0:T(8,128)(2,1)}, u32[]{:S(2)}, u32[]{:S(2)}) collective-permute-start(bf16[1024,768]{1,0:T(8,128)(2,1)} %pad_maximum_fusion), channel_id=1, source_target_pairs={{0,2},{1,3},{2,0},{3,1},{4,6},{5,7},{6,4},{7,5},{8,10},{9,11},{10,... | collective-permute-start | bytes 4718600 | tf_op jit(solution)/shard_map/ppermute | solution.py:166
  416.3 4.6 copy-start.16
  464.2 304.7 %all-reduce.5.cloned.1.call-start = ((), (), s32[]{:S(2)}) async-start(), calls=%async_computation.11 | async-start | bytes 14155776 | tf_op jit(solution)/shard_map/psum | solution.py:205
  464.5 7.2 copy-start.34
  464.5 7.2 copy-start.38
  464.5 11.4 %slice-start = ((s8[6291456]{0:T(1024)(128)(4,1)}), s8[4194304]{0:T(1024)(128)(4,1)S(1)}, s32[]{:S(2)}) async-start(s8[6291456]{0:T(1024)(128)(4,1)} %bitcast.164), calls=%async_computation.12 | async-start | bytes 8388608
  471.7 4.2 copy-start.8
  471.7 4.2 slice-start.1
  471.7 5.8 copy-start.33
  481.4 42.9 %copy-start.5 = (f32[512,768]{1,0:T(8,128)S(1)}, f32[512,768]{1,0:T(8,128)}, u32[]{:S(2)}) copy-start(f32[512,768]{1,0:T(8,128)} %copy-done.4) | copy-start | bytes 4718596
  481.5 45.4 %copy-start.25 = (f32[768]{0:T(1024)S(1)}, f32[768]{0:T(1024)}, u32[]{:S(2)}) copy-start(f32[768]{0:T(1024)} %get-tuple-element.136) | copy-start | bytes 9220
  481.5 45.4 %copy-start.26 = (f32[768]{0:T(1024)S(1)}, f32[768]{0:T(1024)}, u32[]{:S(2)}) copy-start(f32[768]{0:T(1024)} %get-tuple-element.139) | copy-start | bytes 9220
  481.5 45.3 %copy-start.27 = (f32[768]{0:T(1024)S(1)}, f32[768]{0:T(1024)}, u32[]{:S(2)}) copy-start(f32[768]{0:T(1024)} %get-tuple-element.211) | copy-start | bytes 9220
  768.9 5.9 copy-start.14
  768.9 6.7 copy-start.13
  (19 other events, 31.4 us)
Sparse Core Ops, SparseCore 0:
  9.6 31.2 all-gather.3
  74.4 58.3 reduce-scatter.4
  136.9 28.5 all-gather.5
  190.3 58.3 reduce-scatter.6
  256.9 28.5 all-gather.7
  302.8 58.3 reduce-scatter.8
  464.4 59.8 reduce-scatter.10
  530.5 238.3 all-reduce.4
